TPU v7x, 128 devices: a whole 4x4x4 slice. The times are simulated.
128 devices in a mesh: lat: 8 (over x_lo, y), lon: 16 (over z, x_hi, core).
Axes of the slice: x: 4 (x_hi: 2, x_lo: 2; x = x_hi * 2 + x_lo), y: 4, z: 4, core: 2. Of those that a mesh axis runs over, the one named last changes fastest.
Arguments:
- grad_rows: bfloat16 [131072, 128], P(('lat', 'lon')), may hold values from -6 to 6
- owner: int32 [131072, 1], P(('lat', 'lon')), may hold values from 0 to 127; in each aligned block of 1024 rows (0 to 1023, 1024 to 2047, ...) at most 16 rows name the same one
- lat_offset: int32 [131072], P(('lat', 'lon')), may hold values from 0 to 63
- lon_offset: int32 [131072], P(('lat', 'lon')), may hold values from 0 to 127
- position: bfloat16 [131072, 2], P(('lat', 'lon')), may hold values from 0 to 1
- live_count: int32 [128], P(('lat', 'lon')), may hold values from 512 to 1024
- features: bfloat16 [512, 2048, 128], P('lat', 'lon'), may hold values from -6 to 6
- conv_weight: bfloat16 [3, 3, 128, 128], replicated, may hold values from -0.1875 to 0.1875
Outputs:
- input_grad: bfloat16 [512, 2048, 128], P('lat', 'lon')
- weight_grad: float32 [3, 3, 128, 128], replicated
Inputs may be any that keep to these rules, and one draw needn't show every extreme that they name: `owner`: among the 1024 rows of one device no tile is named more than 16 times, a bound that some block reaches. `live_count`: entry k counts the real rows among the rows of device k, which come first.
All inputs are finite; a program needn't handle non-finite values.
Results may differ from a plain program's by a relative error of at most 0.012.
Values may be sent and summed in bfloat16 or wider, within the bound.
No kernel may reach another device: no remote copies, remote signals or barrier semaphores. Data moves between devices by JAX's collectives and lax.ppermute only.
A program may use at most 128 MiB of HBM per device.

v0:
```python
import math
import jax
import jax.numpy as jnp
from jax import lax
from jax.sharding import PartitionSpec as P

rbf_scale = 1.5


def padded_2(cells, sides, width, closed):
    for axis, dim in sides:
        count = lax.axis_size(axis)
        ends = count if closed else count - 1
        head = lax.slice_in_dim(cells, 0, width, axis=dim)
        tail = lax.slice_in_dim(cells, cells.shape[dim] - width, cells.shape[dim], axis=dim)
        cells = jnp.concatenate(
            [
                lax.ppermute(tail, axis, [(i, (i + 1) % count) for i in range(ends)]),
                cells,
                lax.ppermute(head, axis, [((i + 1) % count, i) for i in range(ends)]),
            ],
            axis=dim,
        )
    return cells


def cut_along(value, dim, count):
    before, after = (value.shape[:dim], value.shape[dim + 1 :])
    return jnp.moveaxis(value.reshape(*before, count, -1, *after), dim, 0)


def in_order(parts, dim):
    shape = list(parts.shape[1:])
    shape[dim] *= parts.shape[0]
    return jnp.moveaxis(parts, 0, dim).reshape(shape)


def one_exchange(value, axis, axes, splits, concats):
    sizes = [lax.axis_size(a) for a in axes]
    parts = cut_along(value, splits[0], sizes[0])
    parts = jnp.moveaxis(cut_along(parts, splits[1] + 1, sizes[1]), 0, 1)
    inside = parts.shape[2:]
    parts = parts.reshape(-1, *inside)
    parts = lax.all_to_all(parts, axis, split_axis=0, concat_axis=0, tiled=True)
    parts = in_order(parts.reshape(*sizes, *inside), concats[0] + 1)
    return in_order(parts, concats[1])


def profile(frac):
    tap_index = jnp.arange(8).astype(frac.dtype)
    return jnp.exp(
        -jnp.square(tap_index[None, :] - 3.0 - frac[:, None]) / (2.0 * rbf_scale * rbf_scale)
    )


def clear_rim(padded):
    lat_index = lax.axis_index("lat")
    lat_count = lax.axis_size("lat")
    row_line = jnp.arange(padded.shape[0], dtype=jnp.int32)
    masked = (row_line == 0) & (lat_index == 0) | (row_line == padded.shape[0] - 1) & (
        lat_index == lat_count - 1
    )
    return jnp.where(masked[:, None, None], jnp.zeros_like(padded), padded)


def tap_matrix(offsets, weights, extent):
    tap_ints = jnp.arange(8, dtype=jnp.int32)
    cells = offsets[:, None] + tap_ints[None, :] + 1
    line = jnp.arange(extent, dtype=jnp.int32)
    picked = jnp.where(
        cells[:, :, None] == line[None, None, :], weights.astype(jnp.float32)[:, :, None], 0.0
    )
    return jnp.sum(picked, axis=1).astype(jnp.bfloat16)


def shards(grad_rows, owner, lat_offset, lon_offset, position, live_count, features, conv_weight):
    lat_total = lax.axis_size("lat")
    lon_total = lax.axis_size("lon")
    device_total = lat_total * lon_total
    row_total = grad_rows.shape[0]
    channels = grad_rows.shape[1]
    tile_lat = features.shape[0]
    tile_lon = features.shape[1]
    capacity = max(2, 2 * row_total // device_total)
    input_padded = clear_rim(padded_2(features, (("lat", 0), ("lon", 1)), 1, True))
    owner_tile = owner[:, 0]
    is_live = jnp.arange(row_total, dtype=jnp.int32) < live_count[0]
    matches = (
        (owner_tile[:, None] == jnp.arange(device_total, dtype=jnp.int32)[None, :])
        & is_live[:, None]
    ).astype(jnp.int32)
    earlier = jnp.cumsum(matches, axis=0) - matches
    slot_rank = jnp.sum(earlier * matches, axis=1)
    slot_index = jnp.where(is_live, owner_tile * capacity + slot_rank, device_total * capacity)
    outgoing = (
        jnp.zeros((device_total * capacity, channels), jnp.bfloat16)
        .at[slot_index]
        .set(grad_rows, mode="drop")
    )
    geometry = jnp.stack(
        [
            position[:, 0],
            position[:, 1],
            lat_offset.astype(jnp.bfloat16),
            lon_offset.astype(jnp.bfloat16),
        ],
        axis=1,
    )
    place_out = (
        jnp.zeros((device_total * capacity, 4), jnp.bfloat16)
        .at[slot_index]
        .set(geometry, mode="drop")
    )
    incoming, place_in = (
        one_exchange(
            outgoing.reshape(lat_total, lon_total, capacity, channels),
            ("lat", "lon"),
            ("lat", "lon"),
            (0, 1),
            (0, 1),
        ),
        one_exchange(
            place_out.reshape(lat_total, lon_total, capacity, 4),
            ("lat", "lon"),
            ("lat", "lon"),
            (0, 1),
            (0, 1),
        ),
    )
    incoming = incoming.reshape(-1, channels)
    place_in = place_in.reshape(-1, 4).astype(jnp.float32)
    padded_lat = tile_lat + 8
    padded_lon = tile_lon + 8
    slot_total = incoming.shape[0]
    block_rows = math.gcd(slot_total, 256)

    def accumulate(canvas, payload):
        rows_blk, place_blk = payload
        lat_weight = profile(place_blk[:, 0]).astype(jnp.bfloat16)
        lon_weight = profile(place_blk[:, 1]).astype(jnp.bfloat16)
        lat_matrix = tap_matrix(place_blk[:, 2].astype(jnp.int32), lat_weight, padded_lat)
        lon_matrix = tap_matrix(place_blk[:, 3].astype(jnp.int32), lon_weight, padded_lon)
        spread = (lon_matrix[:, :, None] * rows_blk[:, None, :]).reshape(
            rows_blk.shape[0], padded_lon * channels
        )
        canvas = canvas + lax.dot_general(
            lat_matrix, spread, (((0,), (0,)), ((), ())), preferred_element_type=jnp.float32
        )
        return (canvas, None)

    canvas, _ = lax.scan(
        accumulate,
        jnp.zeros((padded_lat, padded_lon * channels), jnp.float32),
        (incoming.reshape(-1, block_rows, channels), place_in.reshape(-1, block_rows, 4)),
    )
    canvas = canvas.reshape(padded_lat, padded_lon, channels)
    edge_rows = jnp.concatenate([canvas[:5], canvas[-5:]], axis=0)
    edge_rows = padded_2(edge_rows.astype(jnp.bfloat16), (("lat", 0),), 5, False).astype(
        edge_rows.dtype
    )
    inner = canvas[4:-4]
    inner = inner.at[:4].add(edge_rows[1:5]).at[-4:].add(edge_rows[15:19])
    rim_top = edge_rows[0] + canvas[3]
    rim_bottom = canvas[-4] + edge_rows[19]
    tall = jnp.concatenate([rim_top[None], inner, rim_bottom[None]], axis=0)
    side_cols = jnp.concatenate([tall[:, :5], tall[:, -5:]], axis=1)
    side_cols = padded_2(side_cols.astype(jnp.bfloat16), (("lon", 1),), 5, True).astype(
        side_cols.dtype
    )
    middle = tall[:, 4:-4]
    middle = middle.at[:, :4].add(side_cols[:, 1:5]).at[:, -4:].add(side_cols[:, 15:19])
    rim_left = side_cols[:, 0] + tall[:, 3]
    rim_right = tall[:, -4] + side_cols[:, 19]
    whole = jnp.concatenate([rim_left[:, None], middle, rim_right[:, None]], axis=1)
    grid_padded = clear_rim(whole.astype(jnp.bfloat16))
    grid_grad = grid_padded[1:-1, 1:-1]
    flat_grad = grid_grad.reshape(-1, channels)
    input_grad = jnp.zeros((tile_lat * tile_lon, channels), jnp.float32)
    weight_parts = []
    for a in range(3):
        for b in range(3):
            shifted = grid_padded[2 - a : 2 - a + tile_lat, 2 - b : 2 - b + tile_lon].reshape(
                -1, channels
            )
            input_grad = input_grad + lax.dot_general(
                shifted,
                conv_weight[a, b],
                (((1,), (1,)), ((), ())),
                preferred_element_type=jnp.float32,
            )
            window = input_padded[a : a + tile_lat, b : b + tile_lon].reshape(-1, channels)
            weight_parts.append(
                lax.dot_general(
                    window, flat_grad, (((0,), (0,)), ((), ())), preferred_element_type=jnp.float32
                )
            )
    weight_grad = lax.psum(
        jnp.stack(weight_parts).reshape(3, 3, channels, channels), ("lat", "lon")
    )
    return (input_grad.reshape(tile_lat, tile_lon, channels).astype(jnp.bfloat16), weight_grad)


def solution(mesh):
    placed = (
        P(("lat", "lon"), None),
        P(("lat", "lon"), None),
        P(("lat", "lon")),
        P(("lat", "lon")),
        P(("lat", "lon"), None),
        P(("lat", "lon")),
        P("lat", "lon", None),
        P(),
    )
    return jax.shard_map(
        shards, mesh=mesh, in_specs=placed, out_specs=(P("lat", "lon", None), P()), check_vma=False
    )
```

profile of v0, /device:TPU:1, one launch (start us, length us, event | category | flops | bytes accessed | tf_op | source)
XLA Modules:
  0.0 357.4 jit_solution(9674923736870181824)
XLA Ops:
  8.0 4.5 %collective-permute-start.5 = (bf16[1,128,128]{2,1,0:T(8,128)(2,1)S(1)}, bf16[1,128,128]{2,1,0:T(8,128)(2,1)S(1)}, u32[]{:S(2)}, u32[]{:S(2)}) collective-permute-start(bf16[1,128,128]{2,1,0:T(8,128)(2,1)S(1)} %get-tuple-element.168), channel_id=1, source_target_pairs={{16,0},{32,16},{48,32},{64,48},{80,64},{96,80},{112,96},{0,112},{1... | collective-permute-start | bytes 98312 | tf_op jit(solution)/shard_map/ppermute | solution.py:20
  17.3 3.3 scatter_custom_fusion
  20.7 1.5 copy.87
  22.2 11.0 %all-to-all-start = ((bf16[128,1,1,16,4]{3,4,2,1,0:T(4,128)(2,1)}), bf16[128,1,1,16,4]{3,4,2,1,0:T(4,128)(2,1)S(1)}, u32[]{:S(2)}, u32[]{:S(2)}) async-start(bf16[128,1,1,16,4]{3,4,2,1,0:T(4,128)(2,1)} %copy.87), calls=%async_computation | async-start | bytes 262144 | tf_op jit(solution)/shard_map/all_to_all | solution.py:44
  33.2 4.3 %scatter_custom_fusion.1 = bf16[2048,128]{1,0:T(8,128)(2,1)} fusion(s32[1024]{0:T(1024)S(1)} %bitcast.226, bf16[1024,128]{1,0:T(8,128)(2,1)} %param.18, bf16[]{:T(256)} %constant.168.clone.1), kind=kCustom, calls=%fused_computation.87 | custom fusion | bytes 524800 | tf_op jit(solution)/shard_map/scatter | solution.py:98
  37.5 5.6 %all-to-all-done = bf16[128,1,1,16,4]{3,4,2,1,0:T(4,128)(2,1)S(1)} async-done(((bf16[128,1,1,16,4]{3,4,2,1,0:T(4,128)(2,1)}), bf16[128,1,1,16,4]{3,4,2,1,0:T(4,128)(2,1)S(1)}, u32[]{:S(2)}, u32[]{:S(2)}) %all-to-all-start) | async-done | bytes 16416 | tf_op jit(solution)/shard_map/all_to_all | solution.py:44
  43.1 4.2 %all-to-all-start.1 = ((bf16[128,1,1,16,128]{4,3,2,1,0:T(8,128)(2,1)}), bf16[128,1,1,16,128]{4,3,2,1,0:T(8,128)(2,1)S(1)}, u32[]{:S(2)}, u32[]{:S(2)}) async-start(bf16[128,1,1,16,128]{4,3,2,1,0:T(8,128)(2,1)} %bitcast.13), calls=%async_computation.1 | async-start | bytes 1048576 | tf_op jit(solution)/shard_map/all_to_all | solution.py:44
  47.9 2.0 constant_dynamic-update-slice_fusion.1
  50.0 3.2 collective-permute-start.6
  53.2 8.2 %all-to-all-done.1 = bf16[128,1,1,16,128]{4,3,2,1,0:T(8,128)(2,1)S(1)} async-done(((bf16[128,1,1,16,128]{4,3,2,1,0:T(8,128)(2,1)}), bf16[128,1,1,16,128]{4,3,2,1,0:T(8,128)(2,1)S(1)}, u32[]{:S(2)}, u32[]{:S(2)}) %all-to-all-start.1) | async-done | bytes 524320 | tf_op jit(solution)/shard_map/all_to_all | solution.py:44
  61.4 91.8 %while.17 = (s32[]{:T(128)}, f32[72,17408]{1,0:T(8,128)}, f32[8,256,4]{1,2,0:T(4,128)S(1)}, bf16[8,256,128]{2,1,0:T(8,128)(2,1)S(1)}, s32[]{:T(128)}, /*index=5*/s32[]{:T(128)}) while((s32[]{:T(128)}, f32[72,17408]{1,0:T(8,128)}, f32[8,256,4]{1,2,0:T(4,128)S(1)}, bf16[8,256,128]{2,1,0:T(8,128)(2,1)S(1)}, s32[]{:T(128)}, ...), condition=%wide.region_8.9_spmd.clone, body=%wide.region_5.8_spmd.clone.sunk | while | flops 649949696 | bytes 63582440 | solution.py:151
  61.9 5.2 %broadcast_multiply_fusion.2 = bf16[256,136,128]{2,1,0:T(8,128)(2,1)S(1)} fusion(bf16[256,128]{1,0:T(8,128)(2,1)S(1)} %dynamic-slice_bitcast_fusion.4, bf16[256,136]{1,0:T(8,128)(2,1)S(1)} %copy.129), kind=kLoop, calls=%fused_computation.5.clone.1 | loop fusion | flops 4456448 | bytes 9048064 | tf_op jit(solution)/shard_map/while/body/eval_jaxpr/mul | solution.py:143
  67.1 3.6 convolution_add_fusion.10
  70.7 2.2 copy-done
  73.4 5.2 %broadcast_multiply_fusion.2 = bf16[256,136,128]{2,1,0:T(8,128)(2,1)S(1)} fusion(bf16[256,128]{1,0:T(8,128)(2,1)S(1)} %dynamic-slice_bitcast_fusion.4, bf16[256,136]{1,0:T(8,128)(2,1)S(1)} %copy.129), kind=kLoop, calls=%fused_computation.5.clone.1 | loop fusion | flops 4456448 | bytes 9048064 | tf_op jit(solution)/shard_map/while/body/eval_jaxpr/mul | solution.py:143
  78.6 3.6 convolution_add_fusion.10
  82.2 2.2 copy-done
  84.8 5.2 %broadcast_multiply_fusion.2 = bf16[256,136,128]{2,1,0:T(8,128)(2,1)S(1)} fusion(bf16[256,128]{1,0:T(8,128)(2,1)S(1)} %dynamic-slice_bitcast_fusion.4, bf16[256,136]{1,0:T(8,128)(2,1)S(1)} %copy.129), kind=kLoop, calls=%fused_computation.5.clone.1 | loop fusion | flops 4456448 | bytes 9048064 | tf_op jit(solution)/shard_map/while/body/eval_jaxpr/mul | solution.py:143
  90.1 3.6 convolution_add_fusion.10
  93.6 2.2 copy-done
  96.3 5.2 %broadcast_multiply_fusion.2 = bf16[256,136,128]{2,1,0:T(8,128)(2,1)S(1)} fusion(bf16[256,128]{1,0:T(8,128)(2,1)S(1)} %dynamic-slice_bitcast_fusion.4, bf16[256,136]{1,0:T(8,128)(2,1)S(1)} %copy.129), kind=kLoop, calls=%fused_computation.5.clone.1 | loop fusion | flops 4456448 | bytes 9048064 | tf_op jit(solution)/shard_map/while/body/eval_jaxpr/mul | solution.py:143
  101.5 3.6 convolution_add_fusion.10
  105.1 2.2 copy-done
  107.8 5.2 %broadcast_multiply_fusion.2 = bf16[256,136,128]{2,1,0:T(8,128)(2,1)S(1)} fusion(bf16[256,128]{1,0:T(8,128)(2,1)S(1)} %dynamic-slice_bitcast_fusion.4, bf16[256,136]{1,0:T(8,128)(2,1)S(1)} %copy.129), kind=kLoop, calls=%fused_computation.5.clone.1 | loop fusion | flops 4456448 | bytes 9048064 | tf_op jit(solution)/shard_map/while/body/eval_jaxpr/mul | solution.py:143
  113.0 3.6 convolution_add_fusion.10
  116.6 2.2 copy-done
  119.3 5.2 %broadcast_multiply_fusion.2 = bf16[256,136,128]{2,1,0:T(8,128)(2,1)S(1)} fusion(bf16[256,128]{1,0:T(8,128)(2,1)S(1)} %dynamic-slice_bitcast_fusion.4, bf16[256,136]{1,0:T(8,128)(2,1)S(1)} %copy.129), kind=kLoop, calls=%fused_computation.5.clone.1 | loop fusion | flops 4456448 | bytes 9048064 | tf_op jit(solution)/shard_map/while/body/eval_jaxpr/mul | solution.py:143
  124.5 3.6 convolution_add_fusion.10
  128.1 2.2 copy-done
  130.8 5.2 %broadcast_multiply_fusion.2 = bf16[256,136,128]{2,1,0:T(8,128)(2,1)S(1)} fusion(bf16[256,128]{1,0:T(8,128)(2,1)S(1)} %dynamic-slice_bitcast_fusion.4, bf16[256,136]{1,0:T(8,128)(2,1)S(1)} %copy.129), kind=kLoop, calls=%fused_computation.5.clone.1 | loop fusion | flops 4456448 | bytes 9048064 | tf_op jit(solution)/shard_map/while/body/eval_jaxpr/mul | solution.py:143
  136.0 3.6 convolution_add_fusion.10
  139.5 2.2 copy-done
  142.2 5.2 %broadcast_multiply_fusion.2 = bf16[256,136,128]{2,1,0:T(8,128)(2,1)S(1)} fusion(bf16[256,128]{1,0:T(8,128)(2,1)S(1)} %dynamic-slice_bitcast_fusion.4, bf16[256,136]{1,0:T(8,128)(2,1)S(1)} %copy.129), kind=kLoop, calls=%fused_computation.5.clone.1 | loop fusion | flops 4456448 | bytes 9048064 | tf_op jit(solution)/shard_map/while/body/eval_jaxpr/mul | solution.py:143
  147.4 3.6 convolution_add_fusion.10
  151.0 2.2 copy-done
  153.2 1.3 fusion.128
  154.6 2.8 convert.27
  157.4 1.1 copy-done.1
  159.8 1.3 collective-permute-start.1
  161.1 4.0 %collective-permute-start = (bf16[5,136,128]{2,1,0:T(8,128)(2,1)S(1)}, bf16[5,136,128]{2,1,0:T(8,128)(2,1)S(1)}, u32[]{:S(2)}, u32[]{:S(2)}) collective-permute-start(bf16[5,136,128]{2,1,0:T(8,128)(2,1)S(1)} %bitcast.203), channel_id=1, source_target_pairs={{0,16},{16,32},{32,48},{48,64},{64,80},{80,96},{96,112},{1,17},{17... | collective-permute-start | bytes 522248 | tf_op jit(solution)/shard_map/ppermute | solution.py:18
  165.2 2.3 collective-permute-done.1
  167.4 0.9 collective-permute-done
  168.8 2.0 collective-permute-start.2
  171.7 1.1 collective-permute-done.2
  172.8 4.2 %collective-permute-done.3 = bf16[66,5,128]{2,1,0:T(8,128)(2,1)S(1)} collective-permute-done((bf16[66,5,128]{2,1,0:T(8,128)(2,1)S(1)}, bf16[66,5,128]{2,1,0:T(8,128)(2,1)S(1)}, u32[]{:S(2)}, u32[]{:S(2)}) %collective-permute-start.3) | collective-permute-done | bytes 84512 | tf_op jit(solution)/shard_map/ppermute | solution.py:20
  178.0 3.1 maximum_select_fusion.1
  181.1 7.0 %fusion.129 = (bf16[64,128,128]{2,1,0:T(8,128)(2,1)}, bf16[64,128,128]{2,1,0:T(8,128)(2,1)S(1)}, bf16[64,128,128]{2,1,0:T(8,128)(2,1)}, bf16[64,128,128]{2,1,0:T...) fusion(bf16[66,130,128]{2,1,0:T(8,128)(2,1)S(1)} %get-tuple-ele, ...), kind=kLoop, calls=%fused_computation.153 | loop fusion | bytes 37748736 | tf_op jit(solution)/shard_map/slice | solution.py:182
  189.0 1.3 fusion.33
  190.3 1.3 fusion.39
  192.5 1.3 fusion.51
  193.8 1.3 fusion.57
  195.2 0.8 fusion.63
  196.0 1.3 fusion.69
  197.3 1.3 fusion.75
  199.5 2.4 fusion.107
  202.7 0.9 copy-done.6
  204.3 0.9 copy-done.5
  205.2 1.0 convolution_add_fusion.6
  207.5 0.9 copy-done.3
  209.1 0.9 copy-done.2
  211.4 0.9 copy-done.8
  212.3 2.0 fusion.5
  214.3 134.3 %all-reduce.2.cloned.1.call-done = f32[3,3,128,128]{3,2,1,0:T(8,128)} async-done(((f32[3,3,128,128]{3,2,1,0:T(8,128)}), f32[3,3,128,128]{3,2,1,0:T(8,128)}) %all-reduce.2.cloned.1.call-update) | async-done | bytes 589840 | tf_op jit(solution)/shard_map/psum | solution.py:197
  348.6 1.9 copy.152
  (205 shorter events, 19.9 us)
Async XLA Ops:
  7.2 9.6 %copy-start.11 = (s32[1024,1]{0,1:T(1,128)S(1)}, s32[1024,1]{0,1:T(1,128)}, u32[]{:S(2)}) copy-start(s32[1024,1]{0,1:T(1,128)} %param.19) | copy-start | bytes 12292
  8.0 41.9 %collective-permute-start.5 = (bf16[1,128,128]{2,1,0:T(8,128)(2,1)S(1)}, bf16[1,128,128]{2,1,0:T(8,128)(2,1)S(1)}, u32[]{:S(2)}, u32[]{:S(2)}) collective-permute-start(bf16[1,128,128]{2,1,0:T(8,128)(2,1)S(1)} %get-tuple-element.168), channel_id=1, source_target_pairs={{16,0},{32,16},{48,32},{64,48},{80,64},{96,80},{112,96},{0,112},{1... | collective-permute-start | bytes 98312 | tf_op jit(solution)/shard_map/ppermute | solution.py:20
  12.5 35.4 %collective-permute-start.4 = (bf16[1,128,128]{2,1,0:T(8,128)(2,1)S(1)}, bf16[1,128,128]{2,1,0:T(8,128)(2,1)S(1)}, u32[]{:S(2)}, u32[]{:S(2)}) collective-permute-start(bf16[1,128,128]{2,1,0:T(8,128)(2,1)S(1)} %get-tuple-element.169), channel_id=1, source_target_pairs={{0,16},{16,32},{32,48},{48,64},{64,80},{80,96},{96,112},{112,0},{1... | collective-permute-start | bytes 98312 | tf_op jit(solution)/shard_map/ppermute | solution.py:18
  22.2 20.9 %all-to-all-start = ((bf16[128,1,1,16,4]{3,4,2,1,0:T(4,128)(2,1)}), bf16[128,1,1,16,4]{3,4,2,1,0:T(4,128)(2,1)S(1)}, u32[]{:S(2)}, u32[]{:S(2)}) async-start(bf16[128,1,1,16,4]{3,4,2,1,0:T(4,128)(2,1)} %copy.87), calls=%async_computation | async-start | bytes 262144 | tf_op jit(solution)/shard_map/all_to_all | solution.py:44
  43.1 18.3 %all-to-all-start.1 = ((bf16[128,1,1,16,128]{4,3,2,1,0:T(8,128)(2,1)}), bf16[128,1,1,16,128]{4,3,2,1,0:T(8,128)(2,1)S(1)}, u32[]{:S(2)}, u32[]{:S(2)}) async-start(bf16[128,1,1,16,128]{4,3,2,1,0:T(8,128)(2,1)} %bitcast.13), calls=%async_computation.1 | async-start | bytes 1048576 | tf_op jit(solution)/shard_map/all_to_all | solution.py:44
  47.3 301.3 %all-reduce.2.cloned.1.call-start = ((), (), s32[]{:S(2)}) async-start(), calls=%async_computation.2 | async-start | bytes 1179648 | tf_op jit(solution)/shard_map/psum | solution.py:197
  50.0 128.0 %collective-permute-start.6 = (bf16[66,1,128]{2,1,0:T(2,128)(2,1)S(1)}, bf16[66,1,128]{2,1,0:T(2,128)(2,1)S(1)}, u32[]{:S(2)}, u32[]{:S(2)}) collective-permute-start(bf16[66,1,128]{2,1,0:T(2,128)(2,1)S(1)} %get-tuple-element.166), channel_id=1, source_target_pairs={{0,1},{1,2},{2,3},{3,4},{4,5},{5,6},{6,7},{7,8},{8,9},{9,10},{10,1... | collective-permute-start | bytes 50696 | tf_op jit(solution)/shard_map/ppermute | solution.py:18
  53.2 124.8 %collective-permute-start.7 = (bf16[66,1,128]{2,1,0:T(2,128)(2,1)S(1)}, bf16[66,1,128]{2,1,0:T(2,128)(2,1)S(1)}, u32[]{:S(2)}, u32[]{:S(2)}) collective-permute-start(bf16[66,1,128]{2,1,0:T(2,128)(2,1)S(1)} %get-tuple-element.167), channel_id=1, source_target_pairs={{1,0},{2,1},{3,2},{4,3},{5,4},{6,5},{7,6},{8,7},{9,8},{10,9},{11,1... | collective-permute-start | bytes 50696 | tf_op jit(solution)/shard_map/ppermute | solution.py:20
  61.8 5.2 %slice-start = ((s8[5013504]{0:T(1024)(128)(4,1)}), s8[4194304]{0:T(1024)(128)(4,1)S(1)}, s32[]{:S(2)}) async-start(s8[5013504]{0:T(1024)(128)(4,1)} %bitcast.191), calls=%async_computation.3 | async-start | bytes 8388608 | tf_op jit(solution)/shard_map/while
  61.9 5.2 %slice-start.1 = ((s8[5013504]{0:T(1024)(128)(4,1)}), s8[819200]{0:T(1024)(128)(4,1)S(1)}, s32[]{:S(2)}) async-start(s8[5013504]{0:T(1024)(128)(4,1)} %bitcast.191), calls=%async_computation.4 | async-start | bytes 1638400 | tf_op jit(solution)/shard_map/while
  70.7 2.2 copy-start
  73.3 5.2 %slice-start = ((s8[5013504]{0:T(1024)(128)(4,1)}), s8[4194304]{0:T(1024)(128)(4,1)S(1)}, s32[]{:S(2)}) async-start(s8[5013504]{0:T(1024)(128)(4,1)} %bitcast.191), calls=%async_computation.3 | async-start | bytes 8388608 | tf_op jit(solution)/shard_map/while
  73.4 5.2 %slice-start.1 = ((s8[5013504]{0:T(1024)(128)(4,1)}), s8[819200]{0:T(1024)(128)(4,1)S(1)}, s32[]{:S(2)}) async-start(s8[5013504]{0:T(1024)(128)(4,1)} %bitcast.191), calls=%async_computation.4 | async-start | bytes 1638400 | tf_op jit(solution)/shard_map/while
  82.1 2.2 copy-start
  84.8 5.2 %slice-start = ((s8[5013504]{0:T(1024)(128)(4,1)}), s8[4194304]{0:T(1024)(128)(4,1)S(1)}, s32[]{:S(2)}) async-start(s8[5013504]{0:T(1024)(128)(4,1)} %bitcast.191), calls=%async_computation.3 | async-start | bytes 8388608 | tf_op jit(solution)/shard_map/while
  84.8 5.2 %slice-start.1 = ((s8[5013504]{0:T(1024)(128)(4,1)}), s8[819200]{0:T(1024)(128)(4,1)S(1)}, s32[]{:S(2)}) async-start(s8[5013504]{0:T(1024)(128)(4,1)} %bitcast.191), calls=%async_computation.4 | async-start | bytes 1638400 | tf_op jit(solution)/shard_map/while
  93.6 2.2 copy-start
  96.3 5.2 %slice-start = ((s8[5013504]{0:T(1024)(128)(4,1)}), s8[4194304]{0:T(1024)(128)(4,1)S(1)}, s32[]{:S(2)}) async-start(s8[5013504]{0:T(1024)(128)(4,1)} %bitcast.191), calls=%async_computation.3 | async-start | bytes 8388608 | tf_op jit(solution)/shard_map/while
  96.3 5.2 %slice-start.1 = ((s8[5013504]{0:T(1024)(128)(4,1)}), s8[819200]{0:T(1024)(128)(4,1)S(1)}, s32[]{:S(2)}) async-start(s8[5013504]{0:T(1024)(128)(4,1)} %bitcast.191), calls=%async_computation.4 | async-start | bytes 1638400 | tf_op jit(solution)/shard_map/while
  105.1 2.2 copy-start
  107.8 5.2 %slice-start = ((s8[5013504]{0:T(1024)(128)(4,1)}), s8[4194304]{0:T(1024)(128)(4,1)S(1)}, s32[]{:S(2)}) async-start(s8[5013504]{0:T(1024)(128)(4,1)} %bitcast.191), calls=%async_computation.3 | async-start | bytes 8388608 | tf_op jit(solution)/shard_map/while
  107.8 5.2 %slice-start.1 = ((s8[5013504]{0:T(1024)(128)(4,1)}), s8[819200]{0:T(1024)(128)(4,1)S(1)}, s32[]{:S(2)}) async-start(s8[5013504]{0:T(1024)(128)(4,1)} %bitcast.191), calls=%async_computation.4 | async-start | bytes 1638400 | tf_op jit(solution)/shard_map/while
  116.6 2.2 copy-start
  119.2 5.2 %slice-start = ((s8[5013504]{0:T(1024)(128)(4,1)}), s8[4194304]{0:T(1024)(128)(4,1)S(1)}, s32[]{:S(2)}) async-start(s8[5013504]{0:T(1024)(128)(4,1)} %bitcast.191), calls=%async_computation.3 | async-start | bytes 8388608 | tf_op jit(solution)/shard_map/while
  119.3 5.2 %slice-start.1 = ((s8[5013504]{0:T(1024)(128)(4,1)}), s8[819200]{0:T(1024)(128)(4,1)S(1)}, s32[]{:S(2)}) async-start(s8[5013504]{0:T(1024)(128)(4,1)} %bitcast.191), calls=%async_computation.4 | async-start | bytes 1638400 | tf_op jit(solution)/shard_map/while
  128.1 2.2 copy-start
  130.7 5.2 %slice-start = ((s8[5013504]{0:T(1024)(128)(4,1)}), s8[4194304]{0:T(1024)(128)(4,1)S(1)}, s32[]{:S(2)}) async-start(s8[5013504]{0:T(1024)(128)(4,1)} %bitcast.191), calls=%async_computation.3 | async-start | bytes 8388608 | tf_op jit(solution)/shard_map/while
  130.7 5.2 %slice-start.1 = ((s8[5013504]{0:T(1024)(128)(4,1)}), s8[819200]{0:T(1024)(128)(4,1)S(1)}, s32[]{:S(2)}) async-start(s8[5013504]{0:T(1024)(128)(4,1)} %bitcast.191), calls=%async_computation.4 | async-start | bytes 1638400 | tf_op jit(solution)/shard_map/while
  139.5 2.2 copy-start
  142.2 5.2 %slice-start = ((s8[5013504]{0:T(1024)(128)(4,1)}), s8[4194304]{0:T(1024)(128)(4,1)S(1)}, s32[]{:S(2)}) async-start(s8[5013504]{0:T(1024)(128)(4,1)} %bitcast.191), calls=%async_computation.3 | async-start | bytes 8388608 | tf_op jit(solution)/shard_map/while
  142.2 5.2 %slice-start.1 = ((s8[5013504]{0:T(1024)(128)(4,1)}), s8[819200]{0:T(1024)(128)(4,1)S(1)}, s32[]{:S(2)}) async-start(s8[5013504]{0:T(1024)(128)(4,1)} %bitcast.191), calls=%async_computation.4 | async-start | bytes 1638400 | tf_op jit(solution)/shard_map/while
  151.0 2.2 copy-start
  154.6 3.9 %copy-start.1 = (f32[72,17408]{1,0:T(8,128)S(1)}, f32[72,17408]{1,0:T(8,128)}, u32[]{:S(2)}) copy-start(f32[72,17408]{1,0:T(8,128)} %get-tuple-element.103) | copy-start | bytes 15040516
  159.8 7.7 %collective-permute-start.1 = (bf16[5,136,128]{2,1,0:T(8,128)(2,1)S(1)}, bf16[5,136,128]{2,1,0:T(8,128)(2,1)S(1)}, u32[]{:S(2)}, u32[]{:S(2)}) collective-permute-start(bf16[5,136,128]{2,1,0:T(8,128)(2,1)S(1)} %bitcast.207), channel_id=1, source_target_pairs={{16,0},{32,16},{48,32},{64,48},{80,64},{96,80},{112,96},{17,1},{33... | collective-permute-start | bytes 522248 | tf_op jit(solution)/shard_map/ppermute | solution.py:20
  161.1 7.2 %collective-permute-start = (bf16[5,136,128]{2,1,0:T(8,128)(2,1)S(1)}, bf16[5,136,128]{2,1,0:T(8,128)(2,1)S(1)}, u32[]{:S(2)}, u32[]{:S(2)}) collective-permute-start(bf16[5,136,128]{2,1,0:T(8,128)(2,1)S(1)} %bitcast.203), channel_id=1, source_target_pairs={{0,16},{16,32},{32,48},{48,64},{64,80},{80,96},{96,112},{1,17},{17... | collective-permute-start | bytes 522248 | tf_op jit(solution)/shard_map/ppermute | solution.py:18
  168.8 3.9 %collective-permute-start.2 = (bf16[66,5,128]{2,1,0:T(8,128)(2,1)S(1)}, bf16[66,5,128]{2,1,0:T(8,128)(2,1)S(1)}, u32[]{:S(2)}, u32[]{:S(2)}) collective-permute-start(bf16[66,5,128]{2,1,0:T(8,128)(2,1)S(1)} %get-tuple-element.164), channel_id=1, source_target_pairs={{0,1},{1,2},{2,3},{3,4},{4,5},{5,6},{6,7},{7,8},{8,9},{9,10},{10,1... | collective-permute-start | bytes 253448 | tf_op jit(solution)/shard_map/ppermute | solution.py:18
  170.8 6.2 %collective-permute-start.3 = (bf16[66,5,128]{2,1,0:T(8,128)(2,1)S(1)}, bf16[66,5,128]{2,1,0:T(8,128)(2,1)S(1)}, u32[]{:S(2)}, u32[]{:S(2)}) collective-permute-start(bf16[66,5,128]{2,1,0:T(8,128)(2,1)S(1)} %get-tuple-element.165), channel_id=1, source_target_pairs={{1,0},{2,1},{3,2},{4,3},{5,4},{6,5},{7,6},{8,7},{9,8},{10,9},{11,1... | collective-permute-start | bytes 253448 | tf_op jit(solution)/shard_map/ppermute | solution.py:20
  197.3 2.2 copy-start.10
  198.7 0.8 copy-start.9
  199.5 2.5 copy-start.7
  202.0 1.6 copy-start.6
  203.6 1.6 copy-start.5
  205.2 1.6 copy-start.4
  206.8 1.6 copy-start.3
  208.4 1.6 copy-start.2
  210.7 1.6 copy-start.8
Sparse Core Ops, SparseCore 0:
  199.6 148.9 all-reduce.1
where the time goes:
time: 358 us; the launch traced here: 357 us
  waiting for transfers between devices  157 us (44%)
  other arithmetic  54.3 us (15%)
  local copies, waits for them, and re-layouts  51.6 us (14%)
  matrix products  48.7 us (14%)
  starting transfers between devices  30.1 us (8%)
  between operations  15.2 us (4%)
    psum x1, waiting for transfers between devices, shards(): lax.psum(jnp.stack(weight_parts).reshape(3, 3, channels, channels), ('lat...  134 us
    mul x8, other arithmetic, accumulate(): lon_matrix[:, :, None] * rows_blk[:, None, :]  41.4 us
    dot_general x8, matrix products, accumulate(): lax.dot_general(lat_matrix, spread, (((0,), (0,)), ((), ())), preferred_e...  28.5 us
    while x48, local copies, waits for them, and re-layouts  17.9 us
    all_to_all x2, starting transfers between devices, one_exchange(): parts = lax.all_to_all(parts, axis, split_axis=0, concat_axis=0, tiled=True)  15.1 us
    all_to_all x2, waiting for transfers between devices, one_exchange(): parts = lax.all_to_all(parts, axis, split_axis=0, concat_axis=0, tiled=True)  13.8 us
    unnamed x33, local copies, waits for them, and re-layouts  12.4 us
    dot_general x9, matrix products, shards(): lax.dot_general(window, flat_grad, (((0,), (0,)), ((), ())), preferred_el...  10.5 us
  transfers between devices with their start and end apart: 11, of which 7 were waited for; matrix products, arithmetic and copies ran while one was open for 30% of the time, Pallas kernels for 0%

commit v1 on v0

--- a/solution.py
+++ b/solution.py
@@ -195,7 +195,7 @@
                 )
             )
     weight_grad = lax.psum(
-        jnp.stack(weight_parts).reshape(3, 3, channels, channels), ("lat", "lon")
+        lax.psum(jnp.stack(weight_parts).reshape(3, 3, channels, channels), "lon"), "lat"
     )
     return (input_grad.reshape(tile_lat, tile_lon, channels).astype(jnp.bfloat16), weight_grad)
 

time: 358 us -> 426 us (1.19); the launches traced: 357 us -> 421 us
  waiting for transfers between devices: 157 us -> 216 us
    psum x1 -> x2, waiting for transfers between devices: 134 us -> 194 us  [the longest x1 126 us: shards(): lax.psum(jnp.stack(weight_parts).reshape(3, 3, channels, channels), 'lon')]
  transfers between devices with their start and end apart: 11 -> 12, of which waited for: 7 -> 8; matrix products, arithmetic and copies ran while one was open for 30% -> 26% of each run, Pallas kernels for 0% -> 0%
where the time goes in v1:
time: 426 us; the launch traced here: 421 us
  waiting for transfers between devices  216 us (51%)
  other arithmetic  54.3 us (13%)
  matrix products  52.7 us (12%)
  local copies, waits for them, and re-layouts  51 us (12%)
  starting transfers between devices  30.4 us (7%)
  between operations  15.2 us (4%)
    psum x1, waiting for transfers between devices, shards(): lax.psum(jnp.stack(weight_parts).reshape(3, 3, channels, channels), 'lon')  126 us
    psum x1, waiting for transfers between devices, shards(): lax.psum(lax.psum(jnp.stack(weight_parts).reshape(3, 3, channels, channel...  67.8 us
    mul x8, other arithmetic, accumulate(): lon_matrix[:, :, None] * rows_blk[:, None, :]  41.4 us
    dot_general x8, matrix products, accumulate(): lax.dot_general(lat_matrix, spread, (((0,), (0,)), ((), ())), preferred_e...  28.5 us
    while x48, local copies, waits for them, and re-layouts  17.9 us
    all_to_all x2, starting transfers between devices, one_exchange(): parts = lax.all_to_all(parts, axis, split_axis=0, concat_axis=0, tiled=True)  15.1 us
    all_to_all x2, waiting for transfers between devices, one_exchange(): parts = lax.all_to_all(parts, axis, split_axis=0, concat_axis=0, tiled=True)  13.8 us
    dot_general x9, matrix products, shards(): lax.dot_general(shifted, conv_weight[a, b], (((1,), (1,)), ((), ())), pre...  13.7 us
  transfers between devices with their start and end apart: 12, of which 8 were waited for; matrix products, arithmetic and copies ran while one was open for 26% of the time, Pallas kernels for 0%

profile of v1, /device:TPU:1, one launch (start us, length us, event | category | flops | bytes accessed | tf_op | source)
XLA Modules:
  0.0 420.6 jit_solution(5465274656484534330)
XLA Ops:
  8.0 4.5 %collective-permute-start.5 = (bf16[1,128,128]{2,1,0:T(8,128)(2,1)S(1)}, bf16[1,128,128]{2,1,0:T(8,128)(2,1)S(1)}, u32[]{:S(2)}, u32[]{:S(2)}) collective-permute-start(bf16[1,128,128]{2,1,0:T(8,128)(2,1)S(1)} %get-tuple-element.168), channel_id=1, source_target_pairs={{16,0},{32,16},{48,32},{64,48},{80,64},{96,80},{112,96},{0,112},{1... | collective-permute-start | bytes 98312 | tf_op jit(solution)/shard_map/ppermute | solution.py:20
  17.3 3.3 scatter_custom_fusion
  20.7 1.5 copy.87
  22.2 11.0 %all-to-all-start = ((bf16[128,1,1,16,4]{3,4,2,1,0:T(4,128)(2,1)}), bf16[128,1,1,16,4]{3,4,2,1,0:T(4,128)(2,1)S(1)}, u32[]{:S(2)}, u32[]{:S(2)}) async-start(bf16[128,1,1,16,4]{3,4,2,1,0:T(4,128)(2,1)} %copy.87), calls=%async_computation | async-start | bytes 262144 | tf_op jit(solution)/shard_map/all_to_all | solution.py:44
  33.2 4.3 %scatter_custom_fusion.1 = bf16[2048,128]{1,0:T(8,128)(2,1)} fusion(s32[1024]{0:T(1024)S(1)} %bitcast.226, bf16[1024,128]{1,0:T(8,128)(2,1)} %param.18, bf16[]{:T(256)} %constant.168.clone.1), kind=kCustom, calls=%fused_computation.87 | custom fusion | bytes 524800 | tf_op jit(solution)/shard_map/scatter | solution.py:98
  37.5 5.6 %all-to-all-done = bf16[128,1,1,16,4]{3,4,2,1,0:T(4,128)(2,1)S(1)} async-done(((bf16[128,1,1,16,4]{3,4,2,1,0:T(4,128)(2,1)}), bf16[128,1,1,16,4]{3,4,2,1,0:T(4,128)(2,1)S(1)}, u32[]{:S(2)}, u32[]{:S(2)}) %all-to-all-start) | async-done | bytes 16416 | tf_op jit(solution)/shard_map/all_to_all | solution.py:44
  43.1 4.2 all-to-all-start.1
  47.9 2.0 constant_dynamic-update-slice_fusion.1
  50.0 3.2 collective-permute-start.6
  53.2 8.2 %all-to-all-done.1 = bf16[128,1,1,16,128]{4,3,2,1,0:T(8,128)(2,1)S(1)} async-done(((bf16[128,1,1,16,128]{4,3,2,1,0:T(8,128)(2,1)}), bf16[128,1,1,16,128]{4,3,2,1,0:T(8,128)(2,1)S(1)}, u32[]{:S(2)}, u32[]{:S(2)}) %all-to-all-start.1) | async-done | bytes 524320 | tf_op jit(solution)/shard_map/all_to_all | solution.py:44
  61.4 91.8 %while.17 = (s32[]{:T(128)}, f32[72,17408]{1,0:T(8,128)}, f32[8,256,4]{1,2,0:T(4,128)S(1)}, bf16[8,256,128]{2,1,0:T(8,128)(2,1)S(1)}, s32[]{:T(128)}, /*index=5*/s32[]{:T(128)}) while((s32[]{:T(128)}, f32[72,17408]{1,0:T(8,128)}, f32[8,256,4]{1,2,0:T(4,128)S(1)}, bf16[8,256,128]{2,1,0:T(8,128)(2,1)S(1)}, s32[]{:T(128)}, ...), condition=%wide.region_8.9_spmd.clone, body=%wide.region_5.8_spmd.clone.sunk | while | flops 649949696 | bytes 63582440 | solution.py:151
  61.9 5.2 %broadcast_multiply_fusion.2 = bf16[256,136,128]{2,1,0:T(8,128)(2,1)S(1)} fusion(bf16[256,128]{1,0:T(8,128)(2,1)S(1)} %dynamic-slice_bitcast_fusion.4, bf16[256,136]{1,0:T(8,128)(2,1)S(1)} %copy.129), kind=kLoop, calls=%fused_computation.5.clone.1 | loop fusion | flops 4456448 | bytes 9048064 | tf_op jit(solution)/shard_map/while/body/eval_jaxpr/mul | solution.py:143
  67.1 3.6 convolution_add_fusion.10
  70.7 2.2 copy-done
  73.4 5.2 %broadcast_multiply_fusion.2 = bf16[256,136,128]{2,1,0:T(8,128)(2,1)S(1)} fusion(bf16[256,128]{1,0:T(8,128)(2,1)S(1)} %dynamic-slice_bitcast_fusion.4, bf16[256,136]{1,0:T(8,128)(2,1)S(1)} %copy.129), kind=kLoop, calls=%fused_computation.5.clone.1 | loop fusion | flops 4456448 | bytes 9048064 | tf_op jit(solution)/shard_map/while/body/eval_jaxpr/mul | solution.py:143
  78.6 3.6 convolution_add_fusion.10
  82.2 2.2 copy-done
  84.8 5.2 %broadcast_multiply_fusion.2 = bf16[256,136,128]{2,1,0:T(8,128)(2,1)S(1)} fusion(bf16[256,128]{1,0:T(8,128)(2,1)S(1)} %dynamic-slice_bitcast_fusion.4, bf16[256,136]{1,0:T(8,128)(2,1)S(1)} %copy.129), kind=kLoop, calls=%fused_computation.5.clone.1 | loop fusion | flops 4456448 | bytes 9048064 | tf_op jit(solution)/shard_map/while/body/eval_jaxpr/mul | solution.py:143
  90.1 3.6 convolution_add_fusion.10
  93.6 2.2 copy-done
  96.3 5.2 %broadcast_multiply_fusion.2 = bf16[256,136,128]{2,1,0:T(8,128)(2,1)S(1)} fusion(bf16[256,128]{1,0:T(8,128)(2,1)S(1)} %dynamic-slice_bitcast_fusion.4, bf16[256,136]{1,0:T(8,128)(2,1)S(1)} %copy.129), kind=kLoop, calls=%fused_computation.5.clone.1 | loop fusion | flops 4456448 | bytes 9048064 | tf_op jit(solution)/shard_map/while/body/eval_jaxpr/mul | solution.py:143
  101.5 3.6 convolution_add_fusion.10
  105.1 2.2 copy-done
  107.8 5.2 %broadcast_multiply_fusion.2 = bf16[256,136,128]{2,1,0:T(8,128)(2,1)S(1)} fusion(bf16[256,128]{1,0:T(8,128)(2,1)S(1)} %dynamic-slice_bitcast_fusion.4, bf16[256,136]{1,0:T(8,128)(2,1)S(1)} %copy.129), kind=kLoop, calls=%fused_computation.5.clone.1 | loop fusion | flops 4456448 | bytes 9048064 | tf_op jit(solution)/shard_map/while/body/eval_jaxpr/mul | solution.py:143
  113.0 3.6 convolution_add_fusion.10
  116.6 2.2 copy-done
  119.3 5.2 %broadcast_multiply_fusion.2 = bf16[256,136,128]{2,1,0:T(8,128)(2,1)S(1)} fusion(bf16[256,128]{1,0:T(8,128)(2,1)S(1)} %dynamic-slice_bitcast_fusion.4, bf16[256,136]{1,0:T(8,128)(2,1)S(1)} %copy.129), kind=kLoop, calls=%fused_computation.5.clone.1 | loop fusion | flops 4456448 | bytes 9048064 | tf_op jit(solution)/shard_map/while/body/eval_jaxpr/mul | solution.py:143
  124.5 3.6 convolution_add_fusion.10
  128.1 2.2 copy-done
  130.8 5.2 %broadcast_multiply_fusion.2 = bf16[256,136,128]{2,1,0:T(8,128)(2,1)S(1)} fusion(bf16[256,128]{1,0:T(8,128)(2,1)S(1)} %dynamic-slice_bitcast_fusion.4, bf16[256,136]{1,0:T(8,128)(2,1)S(1)} %copy.129), kind=kLoop, calls=%fused_computation.5.clone.1 | loop fusion | flops 4456448 | bytes 9048064 | tf_op jit(solution)/shard_map/while/body/eval_jaxpr/mul | solution.py:143
  136.0 3.6 convolution_add_fusion.10
  139.5 2.2 copy-done
  142.2 5.2 %broadcast_multiply_fusion.2 = bf16[256,136,128]{2,1,0:T(8,128)(2,1)S(1)} fusion(bf16[256,128]{1,0:T(8,128)(2,1)S(1)} %dynamic-slice_bitcast_fusion.4, bf16[256,136]{1,0:T(8,128)(2,1)S(1)} %copy.129), kind=kLoop, calls=%fused_computation.5.clone.1 | loop fusion | flops 4456448 | bytes 9048064 | tf_op jit(solution)/shard_map/while/body/eval_jaxpr/mul | solution.py:143
  147.4 3.6 convolution_add_fusion.10
  151.0 2.2 copy-done
  153.2 1.3 fusion.128
  154.6 2.8 convert.27
  157.4 1.1 copy-done.1
  159.8 1.3 collective-permute-start.1
  161.1 4.0 collective-permute-start
  165.2 2.3 collective-permute-done.1
  168.8 2.0 collective-permute-start.2
  171.7 1.1 collective-permute-done.2
  172.8 4.2 %collective-permute-done.3 = bf16[66,5,128]{2,1,0:T(8,128)(2,1)S(1)} collective-permute-done((bf16[66,5,128]{2,1,0:T(8,128)(2,1)S(1)}, bf16[66,5,128]{2,1,0:T(8,128)(2,1)S(1)}, u32[]{:S(2)}, u32[]{:S(2)}) %collective-permute-start.3) | collective-permute-done | bytes 84512 | tf_op jit(solution)/shard_map/ppermute | solution.py:20
  178.0 3.1 maximum_select_fusion.1
  181.1 7.0 %fusion.129 = (bf16[64,128,128]{2,1,0:T(8,128)(2,1)}, bf16[64,128,128]{2,1,0:T(8,128)(2,1)S(1)}, bf16[64,128,128]{2,1,0:T(8,128)(2,1)}, bf16[64,128,128]{2,1,0:T...) fusion(bf16[66,130,128]{2,1,0:T(8,128)(2,1)S(1)} %get-tuple-ele, ...), kind=kLoop, calls=%fused_computation.153 | loop fusion | bytes 37748736 | tf_op jit(solution)/shard_map/slice | solution.py:182
  189.0 1.3 fusion.33
  190.3 1.3 fusion.39
  192.5 1.3 fusion.51
  193.8 1.3 fusion.57
  196.0 1.3 fusion.69
  197.3 1.3 fusion.75
  199.9 2.4 fusion.107
  203.0 0.9 copy-done.6
  204.6 0.9 copy-done.5
  206.2 0.9 copy-done.4
  207.8 0.9 copy-done.3
  209.4 0.9 copy-done.2
  210.3 2.6 convolution_add_fusion.3
  212.9 125.9 %all-reduce.3.cloned.1.call-done = f32[3,3,128,128]{3,2,1,0:T(8,128)} async-done(((f32[3,3,128,128]{3,2,1,0:T(8,128)}), f32[3,3,128,128]{3,2,1,0:T(8,128)}) %all-reduce.3.cloned.1.call-update) | async-done | bytes 589840 | tf_op jit(solution)/shard_map/psum | solution.py:198
  338.9 3.0 convolution_add_fusion.2
  342.0 2.0 fusion.5
  344.0 67.8 %all-reduce.5.cloned.1.call-done = f32[3,3,128,128]{3,2,1,0:T(8,128)} async-done(((f32[3,3,128,128]{3,2,1,0:T(8,128)}), f32[3,3,128,128]{3,2,1,0:T(8,128)}) %all-reduce.5.cloned.1.call-update) | async-done | bytes 589840 | tf_op jit(solution)/shard_map/psum | solution.py:197
  411.8 1.9 copy.153
  (208 shorter events, 20.6 us)
Async XLA Ops:
  7.2 9.6 %copy-start.11 = (s32[1024,1]{0,1:T(1,128)S(1)}, s32[1024,1]{0,1:T(1,128)}, u32[]{:S(2)}) copy-start(s32[1024,1]{0,1:T(1,128)} %param.19) | copy-start | bytes 12292
  8.0 41.9 %collective-permute-start.5 = (bf16[1,128,128]{2,1,0:T(8,128)(2,1)S(1)}, bf16[1,128,128]{2,1,0:T(8,128)(2,1)S(1)}, u32[]{:S(2)}, u32[]{:S(2)}) collective-permute-start(bf16[1,128,128]{2,1,0:T(8,128)(2,1)S(1)} %get-tuple-element.168), channel_id=1, source_target_pairs={{16,0},{32,16},{48,32},{64,48},{80,64},{96,80},{112,96},{0,112},{1... | collective-permute-start | bytes 98312 | tf_op jit(solution)/shard_map/ppermute | solution.py:20
  12.5 35.4 %collective-permute-start.4 = (bf16[1,128,128]{2,1,0:T(8,128)(2,1)S(1)}, bf16[1,128,128]{2,1,0:T(8,128)(2,1)S(1)}, u32[]{:S(2)}, u32[]{:S(2)}) collective-permute-start(bf16[1,128,128]{2,1,0:T(8,128)(2,1)S(1)} %get-tuple-element.169), channel_id=1, source_target_pairs={{0,16},{16,32},{32,48},{48,64},{64,80},{80,96},{96,112},{112,0},{1... | collective-permute-start | bytes 98312 | tf_op jit(solution)/shard_map/ppermute | solution.py:18
  22.2 20.9 %all-to-all-start = ((bf16[128,1,1,16,4]{3,4,2,1,0:T(4,128)(2,1)}), bf16[128,1,1,16,4]{3,4,2,1,0:T(4,128)(2,1)S(1)}, u32[]{:S(2)}, u32[]{:S(2)}) async-start(bf16[128,1,1,16,4]{3,4,2,1,0:T(4,128)(2,1)} %copy.87), calls=%async_computation | async-start | bytes 262144 | tf_op jit(solution)/shard_map/all_to_all | solution.py:44
  43.1 18.3 %all-to-all-start.1 = ((bf16[128,1,1,16,128]{4,3,2,1,0:T(8,128)(2,1)}), bf16[128,1,1,16,128]{4,3,2,1,0:T(8,128)(2,1)S(1)}, u32[]{:S(2)}, u32[]{:S(2)}) async-start(bf16[128,1,1,16,128]{4,3,2,1,0:T(8,128)(2,1)} %bitcast.13), calls=%async_computation.1 | async-start | bytes 1048576 | tf_op jit(solution)/shard_map/all_to_all | solution.py:44
  47.3 291.5 %all-reduce.3.cloned.1.call-start = ((), (), s32[]{:S(2)}) async-start(), calls=%async_computation.2 | async-start | bytes 1179648 | tf_op jit(solution)/shard_map/psum | solution.py:198
  50.0 128.0 %collective-permute-start.6 = (bf16[66,1,128]{2,1,0:T(2,128)(2,1)S(1)}, bf16[66,1,128]{2,1,0:T(2,128)(2,1)S(1)}, u32[]{:S(2)}, u32[]{:S(2)}) collective-permute-start(bf16[66,1,128]{2,1,0:T(2,128)(2,1)S(1)} %get-tuple-element.166), channel_id=1, source_target_pairs={{0,1},{1,2},{2,3},{3,4},{4,5},{5,6},{6,7},{7,8},{8,9},{9,10},{10,1... | collective-permute-start | bytes 50696 | tf_op jit(solution)/shard_map/ppermute | solution.py:18
  53.2 124.8 %collective-permute-start.7 = (bf16[66,1,128]{2,1,0:T(2,128)(2,1)S(1)}, bf16[66,1,128]{2,1,0:T(2,128)(2,1)S(1)}, u32[]{:S(2)}, u32[]{:S(2)}) collective-permute-start(bf16[66,1,128]{2,1,0:T(2,128)(2,1)S(1)} %get-tuple-element.167), channel_id=1, source_target_pairs={{1,0},{2,1},{3,2},{4,3},{5,4},{6,5},{7,6},{8,7},{9,8},{10,9},{11,1... | collective-permute-start | bytes 50696 | tf_op jit(solution)/shard_map/ppermute | solution.py:20
  61.8 5.2 %slice-start = ((s8[5013504]{0:T(1024)(128)(4,1)}), s8[4194304]{0:T(1024)(128)(4,1)S(1)}, s32[]{:S(2)}) async-start(s8[5013504]{0:T(1024)(128)(4,1)} %bitcast.191), calls=%async_computation.4 | async-start | bytes 8388608 | tf_op jit(solution)/shard_map/while
  61.9 5.2 %slice-start.1 = ((s8[5013504]{0:T(1024)(128)(4,1)}), s8[819200]{0:T(1024)(128)(4,1)S(1)}, s32[]{:S(2)}) async-start(s8[5013504]{0:T(1024)(128)(4,1)} %bitcast.191), calls=%async_computation.5 | async-start | bytes 1638400 | tf_op jit(solution)/shard_map/while
  70.7 2.2 copy-start
  73.3 5.2 %slice-start = ((s8[5013504]{0:T(1024)(128)(4,1)}), s8[4194304]{0:T(1024)(128)(4,1)S(1)}, s32[]{:S(2)}) async-start(s8[5013504]{0:T(1024)(128)(4,1)} %bitcast.191), calls=%async_computation.4 | async-start | bytes 8388608 | tf_op jit(solution)/shard_map/while
  73.4 5.2 %slice-start.1 = ((s8[5013504]{0:T(1024)(128)(4,1)}), s8[819200]{0:T(1024)(128)(4,1)S(1)}, s32[]{:S(2)}) async-start(s8[5013504]{0:T(1024)(128)(4,1)} %bitcast.191), calls=%async_computation.5 | async-start | bytes 1638400 | tf_op jit(solution)/shard_map/while
  82.1 2.2 copy-start
  84.8 5.2 %slice-start = ((s8[5013504]{0:T(1024)(128)(4,1)}), s8[4194304]{0:T(1024)(128)(4,1)S(1)}, s32[]{:S(2)}) async-start(s8[5013504]{0:T(1024)(128)(4,1)} %bitcast.191), calls=%async_computation.4 | async-start | bytes 8388608 | tf_op jit(solution)/shard_map/while
  84.8 5.2 %slice-start.1 = ((s8[5013504]{0:T(1024)(128)(4,1)}), s8[819200]{0:T(1024)(128)(4,1)S(1)}, s32[]{:S(2)}) async-start(s8[5013504]{0:T(1024)(128)(4,1)} %bitcast.191), calls=%async_computation.5 | async-start | bytes 1638400 | tf_op jit(solution)/shard_map/while
  93.6 2.2 copy-start
  96.3 5.2 %slice-start = ((s8[5013504]{0:T(1024)(128)(4,1)}), s8[4194304]{0:T(1024)(128)(4,1)S(1)}, s32[]{:S(2)}) async-start(s8[5013504]{0:T(1024)(128)(4,1)} %bitcast.191), calls=%async_computation.4 | async-start | bytes 8388608 | tf_op jit(solution)/shard_map/while
  96.3 5.2 %slice-start.1 = ((s8[5013504]{0:T(1024)(128)(4,1)}), s8[819200]{0:T(1024)(128)(4,1)S(1)}, s32[]{:S(2)}) async-start(s8[5013504]{0:T(1024)(128)(4,1)} %bitcast.191), calls=%async_computation.5 | async-start | bytes 1638400 | tf_op jit(solution)/shard_map/while
  105.1 2.2 copy-start
  107.8 5.2 %slice-start = ((s8[5013504]{0:T(1024)(128)(4,1)}), s8[4194304]{0:T(1024)(128)(4,1)S(1)}, s32[]{:S(2)}) async-start(s8[5013504]{0:T(1024)(128)(4,1)} %bitcast.191), calls=%async_computation.4 | async-start | bytes 8388608 | tf_op jit(solution)/shard_map/while
  107.8 5.2 %slice-start.1 = ((s8[5013504]{0:T(1024)(128)(4,1)}), s8[819200]{0:T(1024)(128)(4,1)S(1)}, s32[]{:S(2)}) async-start(s8[5013504]{0:T(1024)(128)(4,1)} %bitcast.191), calls=%async_computation.5 | async-start | bytes 1638400 | tf_op jit(solution)/shard_map/while
  116.6 2.2 copy-start
  119.2 5.2 %slice-start = ((s8[5013504]{0:T(1024)(128)(4,1)}), s8[4194304]{0:T(1024)(128)(4,1)S(1)}, s32[]{:S(2)}) async-start(s8[5013504]{0:T(1024)(128)(4,1)} %bitcast.191), calls=%async_computation.4 | async-start | bytes 8388608 | tf_op jit(solution)/shard_map/while
  119.3 5.2 %slice-start.1 = ((s8[5013504]{0:T(1024)(128)(4,1)}), s8[819200]{0:T(1024)(128)(4,1)S(1)}, s32[]{:S(2)}) async-start(s8[5013504]{0:T(1024)(128)(4,1)} %bitcast.191), calls=%async_computation.5 | async-start | bytes 1638400 | tf_op jit(solution)/shard_map/while
  128.1 2.2 copy-start
  130.7 5.2 %slice-start = ((s8[5013504]{0:T(1024)(128)(4,1)}), s8[4194304]{0:T(1024)(128)(4,1)S(1)}, s32[]{:S(2)}) async-start(s8[5013504]{0:T(1024)(128)(4,1)} %bitcast.191), calls=%async_computation.4 | async-start | bytes 8388608 | tf_op jit(solution)/shard_map/while
  130.7 5.2 %slice-start.1 = ((s8[5013504]{0:T(1024)(128)(4,1)}), s8[819200]{0:T(1024)(128)(4,1)S(1)}, s32[]{:S(2)}) async-start(s8[5013504]{0:T(1024)(128)(4,1)} %bitcast.191), calls=%async_computation.5 | async-start | bytes 1638400 | tf_op jit(solution)/shard_map/while
  139.5 2.2 copy-start
  142.2 5.2 %slice-start = ((s8[5013504]{0:T(1024)(128)(4,1)}), s8[4194304]{0:T(1024)(128)(4,1)S(1)}, s32[]{:S(2)}) async-start(s8[5013504]{0:T(1024)(128)(4,1)} %bitcast.191), calls=%async_computation.4 | async-start | bytes 8388608 | tf_op jit(solution)/shard_map/while
  142.2 5.2 %slice-start.1 = ((s8[5013504]{0:T(1024)(128)(4,1)}), s8[819200]{0:T(1024)(128)(4,1)S(1)}, s32[]{:S(2)}) async-start(s8[5013504]{0:T(1024)(128)(4,1)} %bitcast.191), calls=%async_computation.5 | async-start | bytes 1638400 | tf_op jit(solution)/shard_map/while
  151.0 2.2 copy-start
  154.6 3.9 copy-start.1
  159.8 7.7 %collective-permute-start.1 = (bf16[5,136,128]{2,1,0:T(8,128)(2,1)S(1)}, bf16[5,136,128]{2,1,0:T(8,128)(2,1)S(1)}, u32[]{:S(2)}, u32[]{:S(2)}) collective-permute-start(bf16[5,136,128]{2,1,0:T(8,128)(2,1)S(1)} %bitcast.207), channel_id=1, source_target_pairs={{16,0},{32,16},{48,32},{64,48},{80,64},{96,80},{112,96},{17,1},{33... | collective-permute-start | bytes 522248 | tf_op jit(solution)/shard_map/ppermute | solution.py:20
  161.1 7.2 %collective-permute-start = (bf16[5,136,128]{2,1,0:T(8,128)(2,1)S(1)}, bf16[5,136,128]{2,1,0:T(8,128)(2,1)S(1)}, u32[]{:S(2)}, u32[]{:S(2)}) collective-permute-start(bf16[5,136,128]{2,1,0:T(8,128)(2,1)S(1)} %bitcast.203), channel_id=1, source_target_pairs={{0,16},{16,32},{32,48},{48,64},{64,80},{80,96},{96,112},{1,17},{17... | collective-permute-start | bytes 522248 | tf_op jit(solution)/shard_map/ppermute | solution.py:18
  168.8 3.9 collective-permute-start.2
  170.8 6.2 %collective-permute-start.3 = (bf16[66,5,128]{2,1,0:T(8,128)(2,1)S(1)}, bf16[66,5,128]{2,1,0:T(8,128)(2,1)S(1)}, u32[]{:S(2)}, u32[]{:S(2)}) collective-permute-start(bf16[66,5,128]{2,1,0:T(8,128)(2,1)S(1)} %get-tuple-element.165), channel_id=1, source_target_pairs={{1,0},{2,1},{3,2},{4,3},{5,4},{6,5},{7,6},{8,7},{9,8},{10,9},{11,1... | collective-permute-start | bytes 253448 | tf_op jit(solution)/shard_map/ppermute | solution.py:20
  197.3 2.5 copy-start.10
  198.7 0.8 copy-start.9
  199.5 212.3 %all-reduce.5.cloned.1.call-start = ((), (), s32[]{:S(2)}) async-start(), calls=%async_computation.3 | async-start | bytes 1179648 | tf_op jit(solution)/shard_map/psum | solution.py:197
  199.8 2.5 copy-start.7
  202.3 1.6 copy-start.6
  203.9 1.6 copy-start.5
  205.5 1.6 copy-start.4
  207.1 1.6 copy-start.3
  208.7 1.6 copy-start.2
  338.9 3.1 copy-start.8
Sparse Core Ops, SparseCore 0:
  199.6 139.1 all-reduce.2
  341.5 70.2 all-reduce.4
